TPU v7x, 256 devices: a whole 4x4x8 slice. The times are simulated.
256 devices in a mesh: row: 16 (over y_lo, x, core), col: 16 (over y_hi, z).
Axes of the slice: x: 4, y: 4 (y_hi: 2, y_lo: 2; y = y_hi * 2 + y_lo), z: 8, core: 2. Of those that a mesh axis runs over, the one named last changes fastest.
Arguments:
- amplitudes: bfloat16 [32, 32, 256, 256], P('row', 'col'), may hold values from -6 to 6
- coulomb: bfloat16 [32, 32, 256, 256], P('row', 'col'), may hold values from -12 to 12
- fit_ov: bfloat16 [1024, 32, 256], P(None, 'col'), may hold values from -0.25 to 0.25
- fit_vv: bfloat16 [16, 256, 256], P('row'), may hold values from -0.5 to 0.5
- eps_occ: float32 [32], replicated, may hold values from -2 to -0.5
- eps_vir: float32 [256], replicated, may hold values from 0.5 to 2.5
Outputs:
- updated: bfloat16 [32, 32, 256, 256], P('row', 'col')
All inputs are finite; a program needn't handle non-finite values.
Results may differ from a plain program's by a relative error of at most 0.009.
Values may be sent and summed in bfloat16 or wider, within the bound.
A program may use at most 64 MiB of HBM per device.

v0:
```python
import jax
import jax.numpy as jnp
from jax import lax
from jax.sharding import PartitionSpec as P

ITERS = 2


def ladder_batch(running, flattened, fitting):

    def add_auxiliary(position, partial_value):
        slab = lax.dynamic_index_in_dim(fitting, position, 0, keepdims=False)
        contracted = jnp.einsum(
            "ac,pcd->pad", slab, flattened, preferred_element_type=jnp.float32
        ).astype(jnp.bfloat16)
        return partial_value + jnp.einsum(
            "pad,bd->pab", contracted, slab, preferred_element_type=jnp.float32
        )

    return lax.fori_loop(0, fitting.shape[0], add_auxiliary, running)


def body(amplitudes, coulomb, fit_ov, fit_vv, eps_occ, eps_vir):
    occ_local = amplitudes.shape[0]
    occ_other = amplitudes.shape[1]
    virtual = amplitudes.shape[2]
    occ_rows = lax.dynamic_slice_in_dim(eps_occ, lax.axis_index("row") * occ_local, occ_local)
    occ_cols = lax.dynamic_slice_in_dim(eps_occ, lax.axis_index("col") * occ_other, occ_other)
    denominator = (
        occ_rows[:, None, None, None]
        + occ_cols[None, :, None, None]
        - eps_vir[None, None, :, None]
        - eps_vir[None, None, None, :]
    )
    current = amplitudes
    for sweep in range(ITERS):
        flattened = current.reshape(occ_local * occ_other, virtual, virtual)
        initial = jnp.zeros((occ_local * occ_other, virtual, virtual), jnp.float32)
        ladder = ladder_batch(initial, flattened, lax.all_gather(fit_vv, "row", axis=0, tiled=True))
        ladder = ladder.reshape(occ_local, occ_other, virtual, virtual)
        partial_value = jnp.einsum(
            "qkc,ikac->qia", fit_ov, current, preferred_element_type=jnp.float32
        )
        cycle_partial = lax.psum(partial_value, "col").astype(jnp.bfloat16)
        cycle_term = jnp.einsum(
            "qia,qjb->ijab", cycle_partial, fit_ov, preferred_element_type=jnp.float32
        ).astype(jnp.bfloat16)
        first_move = lax.all_to_all(cycle_term, "row", split_axis=2, concat_axis=0, tiled=True)
        halfway = lax.all_to_all(first_move, "col", split_axis=0, concat_axis=1, tiled=True)
        flipped = jnp.transpose(halfway, (1, 0, 3, 2))
        returned = lax.all_to_all(flipped, "row", split_axis=0, concat_axis=3, tiled=True)
        summed = (
            coulomb.astype(jnp.float32)
            + ladder
            + cycle_term.astype(jnp.float32)
            + returned.astype(jnp.float32)
        )
        current = (summed / denominator).astype(jnp.bfloat16)
    return current


def solution(mesh):
    in_specs = (
        P("row", "col", None, None),
        P("row", "col", None, None),
        P(None, "col", None),
        P("row", None, None),
        P(),
        P(),
    )
    out_specs = P("row", "col", None, None)
    return jax.shard_map(body, mesh=mesh, in_specs=in_specs, out_specs=out_specs, check_vma=False)
```

profile of v0, /device:TPU:1, one launch (start us, length us, event | category | flops | bytes accessed | tf_op | source)
XLA Modules:
  0.0 368.8 jit_solution(2769847445975461815)
XLA Ops:
  6.5 0.7 all-gather.2.cloned.1.call-update
  7.3 2.1 convolution_bitcast_fusion.1
  9.4 87.9 %all-reduce.2 = bf16[1024,2,256]{2,0,1:T(8,128)(2,1)} all-reduce(f32[1024,2,256]{2,0,1:T(8,128)S(1)} %convolution_bitcast_fusion.1), channel_id=1, replica_groups=mesh['row'=16,'col'=16] {'col'}, use_global_device_ids=true, to_apply=%region_2.3 | all-reduce | flops 524288 | bytes 3145728 | tf_op jit(solution)/shard_map/psum | solution.py:44
  97.3 2.0 fusion.14
  99.3 0.5 copy.39
  99.8 25.3 %all_to_all.90 = bf16[2,2,256,256]{3,1,0,2:T(2,128)(2,1)S(1)} all-to-all(bf16[2,2,256,256]{3,1,0,2:T(2,128)(2,1)S(1)} %copy.39), channel_id=1, replica_groups=mesh['row'=16,'col'=16] {'row'}, dimensions={2} | all-to-all | bytes 1048576 | tf_op jit(solution)/shard_map/all_to_all | solution.py:48
  125.2 0.9 copy.41
  126.1 3.7 %all-to-all-start.1 = ((bf16[32,2,16,256]{3,2,1,0:T(8,128)(2,1)}), bf16[32,2,16,256]{3,2,1,0:T(8,128)(2,1)S(1)}, u32[]{:S(2)}, u32[]{:S(2)}) async-start(bf16[32,2,16,256]{3,2,1,0:T(8,128)(2,1)} %bitcast.10), calls=%async_computation.1 | async-start | bytes 1048576 | tf_op jit(solution)/shard_map/all_to_all | solution.py:49
  129.8 14.2 %all-to-all-done.1 = bf16[32,2,16,256]{3,2,1,0:T(8,128)(2,1)S(1)} async-done(((bf16[32,2,16,256]{3,2,1,0:T(8,128)(2,1)}), bf16[32,2,16,256]{3,2,1,0:T(8,128)(2,1)S(1)}, u32[]{:S(2)}, u32[]{:S(2)}) %all-to-all-start.1) | async-done | bytes 524320 | tf_op jit(solution)/shard_map/all_to_all | solution.py:49
  144.0 0.9 copy.43
  144.9 7.0 %all-to-all-start.2 = ((bf16[32,2,256,16]{2,3,1,0:T(8,128)(2,1)}), bf16[32,2,256,16]{2,3,1,0:T(8,128)(2,1)S(1)}, u32[]{:S(2)}, u32[]{:S(2)}) async-start(bf16[32,2,256,16]{2,3,1,0:T(8,128)(2,1)} %copy.43), calls=%async_computation.2 | async-start | bytes 1048576 | tf_op jit(solution)/shard_map/all_to_all | solution.py:51
  152.1 9.3 %all-to-all-done.2 = bf16[32,2,256,16]{2,3,1,0:T(8,128)(2,1)S(1)} async-done(((bf16[32,2,256,16]{2,3,1,0:T(8,128)(2,1)}), bf16[32,2,256,16]{2,3,1,0:T(8,128)(2,1)S(1)}, u32[]{:S(2)}, u32[]{:S(2)}) %all-to-all-start.2) | async-done | bytes 524320 | tf_op jit(solution)/shard_map/all_to_all | solution.py:51
  161.4 0.1 convert_bitcast_fusion.1
  161.5 1.0 copy.44
  162.6 1.6 copy.45
  164.2 27.4 %while.28 = (s32[]{:T(128)}, f32[4,256,256]{2,1,0:T(8,128)S(1)}, bf16[16,256,256]{2,1,0:T(8,128)(2,1)}, bf16[4,256,256]{2,1,0:T(8,128)(2,1)S(1)}, s32[]{:T(128)}, /*index=5*/s32[]{:T(128)}) while((s32[]{:T(128)}, f32[4,256,256]{2,1,0:T(8,128)S(1)}, bf16[16,256,256]{2,1,0:T(8,128)(2,1)}, bf16[4,256,256]{2,1,0:T(8,128)(2,1)S(1)}, ...), condition=%wide.region_1.2_spmd.clone, body=%wide.region_0.1_spmd.clone.sunk | while | flops 269221888 | bytes 2884687 | solution.py:20
  164.2 1.7 convolution_add_fusion.4
  165.9 1.7 convolution_add_fusion.4
  167.6 1.7 convolution_add_fusion.4
  169.4 1.7 convolution_add_fusion.4
  171.1 1.7 convolution_add_fusion.4
  172.8 1.7 convolution_add_fusion.4
  174.5 1.7 convolution_add_fusion.4
  176.2 1.7 convolution_add_fusion.4
  177.9 1.7 convolution_add_fusion.4
  179.6 1.7 convolution_add_fusion.4
  181.3 1.7 convolution_add_fusion.4
  183.0 1.7 convolution_add_fusion.4
  184.7 1.7 convolution_add_fusion.4
  186.5 1.7 convolution_add_fusion.4
  188.2 1.7 convolution_add_fusion.4
  189.9 1.7 convolution_add_fusion.4
  191.6 1.4 fusion.28
  193.0 0.8 convolution_bitcast_fusion
  193.8 80.7 %all-reduce.3 = bf16[1024,2,256]{0,2,1:T(8,128)(2,1)} all-reduce(f32[1024,2,256]{0,2,1:T(8,128)S(1)} %convolution_bitcast_fusion), channel_id=1, replica_groups=mesh['row'=16,'col'=16] {'col'}, use_global_device_ids=true, to_apply=%region_5.6 | all-reduce | flops 524288 | bytes 3145728 | tf_op jit(solution)/shard_map/psum | solution.py:44
  274.5 2.2 fusion.15
  276.8 0.5 copy.48
  277.3 25.4 %all_to_all.91 = bf16[2,2,256,256]{3,1,0,2:T(2,128)(2,1)S(1)} all-to-all(bf16[2,2,256,256]{3,1,0,2:T(2,128)(2,1)S(1)} %copy.48), channel_id=1, replica_groups=mesh['row'=16,'col'=16] {'row'}, dimensions={2} | all-to-all | bytes 1048576 | tf_op jit(solution)/shard_map/all_to_all | solution.py:48
  302.8 0.9 copy.50
  303.6 5.3 %all-to-all-start.4 = ((bf16[32,2,16,256]{3,2,1,0:T(8,128)(2,1)}), bf16[32,2,16,256]{3,2,1,0:T(8,128)(2,1)S(1)}, u32[]{:S(2)}, u32[]{:S(2)}) async-start(bf16[32,2,16,256]{3,2,1,0:T(8,128)(2,1)} %bitcast.30), calls=%async_computation.4 | async-start | bytes 1048576 | tf_op jit(solution)/shard_map/all_to_all | solution.py:49
  308.9 14.8 %all-to-all-done.4 = bf16[32,2,16,256]{3,2,1,0:T(8,128)(2,1)S(1)} async-done(((bf16[32,2,16,256]{3,2,1,0:T(8,128)(2,1)}), bf16[32,2,16,256]{3,2,1,0:T(8,128)(2,1)S(1)}, u32[]{:S(2)}, u32[]{:S(2)}) %all-to-all-start.4) | async-done | bytes 524320 | tf_op jit(solution)/shard_map/all_to_all | solution.py:49
  323.7 0.9 copy.52
  324.6 6.1 %all-to-all-start.5 = ((bf16[32,2,256,16]{2,3,1,0:T(8,128)(2,1)}), bf16[32,2,256,16]{2,3,1,0:T(8,128)(2,1)S(1)}, u32[]{:S(2)}, u32[]{:S(2)}) async-start(bf16[32,2,256,16]{2,3,1,0:T(8,128)(2,1)} %copy.52), calls=%async_computation.5 | async-start | bytes 1048576 | tf_op jit(solution)/shard_map/all_to_all | solution.py:51
  330.7 27.3 %while.29 = (s32[]{:T(128)}, f32[4,256,256]{2,1,0:T(8,128)S(1)}, bf16[16,256,256]{2,1,0:T(8,128)(2,1)}, bf16[4,256,256]{2,1,0:T(8,128)(2,1)S(1)}, s32[]{:T(128)}, /*index=5*/s32[]{:T(128)}) while((s32[]{:T(128)}, f32[4,256,256]{2,1,0:T(8,128)S(1)}, bf16[16,256,256]{2,1,0:T(8,128)(2,1)}, bf16[4,256,256]{2,1,0:T(8,128)(2,1)S(1)}, ...), condition=%wide.region_4.5_spmd.clone, body=%wide.region_3.4_spmd.clone.sunk | while | flops 269221888 | bytes 2884687 | solution.py:20
  330.7 1.7 convolution_add_fusion.5
  332.4 1.7 convolution_add_fusion.5
  334.1 1.7 convolution_add_fusion.5
  335.9 1.7 convolution_add_fusion.5
  337.6 1.7 convolution_add_fusion.5
  339.3 1.7 convolution_add_fusion.5
  341.0 1.7 convolution_add_fusion.5
  342.7 1.7 convolution_add_fusion.5
  344.4 1.7 convolution_add_fusion.5
  346.1 1.7 convolution_add_fusion.5
  347.8 1.7 convolution_add_fusion.5
  349.5 1.7 convolution_add_fusion.5
  351.2 1.7 convolution_add_fusion.5
  353.0 1.7 convolution_add_fusion.5
  354.7 1.7 convolution_add_fusion.5
  356.4 1.7 convolution_add_fusion.5
  358.1 0.1 convert_bitcast_fusion
  358.2 1.1 copy.53
  359.3 1.6 copy.54
  360.9 1.1 fusion.29
  (30 shorter events, 0.5 us)
Async XLA Ops:
  6.5 157.6 %all-gather.2.cloned.1.call-start = ((), (), s32[]{:S(2)}) async-start(), calls=%async_computation.6 | async-start | bytes 2228224 | tf_op jit(solution)/shard_map/all_gather | solution.py:39
  9.4 87.9 %copy-start.1 = (bf16[1024,2,256]{2,1,0:T(2,128)(2,1)S(1)}, bf16[1024,2,256]{2,1,0:T(2,128)(2,1)}, u32[]{:S(2)}) copy-start(bf16[1024,2,256]{2,1,0:T(2,128)(2,1)} %param.12) | copy-start | bytes 3145732
  99.2 26.8 %copy-start.4 = (bf16[2,2,256,256]{3,2,1,0:T(8,128)(2,1)}, bf16[2,2,256,256]{3,2,1,0:T(8,128)(2,1)S(1)}, u32[]{:S(2)}) copy-start(bf16[2,2,256,256]{3,2,1,0:T(8,128)(2,1)S(1)} %fusion.14) | copy-start | bytes 1572868
  126.1 25.8 %copy-start.8 = (f32[32]{0:T(128)S(1)}, f32[32]{0:T(128)}, u32[]{:S(2)}) copy-start(f32[32]{0:T(128)} %param.14) | copy-start | bytes 388
  126.1 26.0 %copy-start.7 = (f32[256]{0:T(256)S(1)}, f32[256]{0:T(256)}, u32[]{:S(2)}) copy-start(f32[256]{0:T(256)} %param.15) | copy-start | bytes 3076
  126.1 17.9 %all-to-all-start.1 = ((bf16[32,2,16,256]{3,2,1,0:T(8,128)(2,1)}), bf16[32,2,16,256]{3,2,1,0:T(8,128)(2,1)S(1)}, u32[]{:S(2)}, u32[]{:S(2)}) async-start(bf16[32,2,16,256]{3,2,1,0:T(8,128)(2,1)} %bitcast.10), calls=%async_computation.1 | async-start | bytes 1048576 | tf_op jit(solution)/shard_map/all_to_all | solution.py:49
  144.9 16.5 %all-to-all-start.2 = ((bf16[32,2,256,16]{2,3,1,0:T(8,128)(2,1)}), bf16[32,2,256,16]{2,3,1,0:T(8,128)(2,1)S(1)}, u32[]{:S(2)}, u32[]{:S(2)}) async-start(bf16[32,2,256,16]{2,3,1,0:T(8,128)(2,1)} %copy.43), calls=%async_computation.2 | async-start | bytes 1048576 | tf_op jit(solution)/shard_map/all_to_all | solution.py:51
  161.5 2.7 copy-start
  164.2 27.4 %copy-start.3 = (bf16[2,2,256,256]{3,2,1,0:T(8,128)(2,1)S(1)}, bf16[2,2,256,256]{3,2,1,0:T(8,128)(2,1)}, u32[]{:S(2)}) copy-start(bf16[2,2,256,256]{3,2,1,0:T(8,128)(2,1)} %param.11) | copy-start | bytes 1572868
  191.6 1.5 copy-start.2
  276.8 26.9 %copy-start.5 = (bf16[2,2,256,256]{3,2,1,0:T(8,128)(2,1)}, bf16[2,2,256,256]{3,2,1,0:T(8,128)(2,1)S(1)}, u32[]{:S(2)}) copy-start(bf16[2,2,256,256]{3,2,1,0:T(8,128)(2,1)S(1)} %fusion.15) | copy-start | bytes 1572868
  303.6 20.1 %all-to-all-start.4 = ((bf16[32,2,16,256]{3,2,1,0:T(8,128)(2,1)}), bf16[32,2,16,256]{3,2,1,0:T(8,128)(2,1)S(1)}, u32[]{:S(2)}, u32[]{:S(2)}) async-start(bf16[32,2,16,256]{3,2,1,0:T(8,128)(2,1)} %bitcast.30), calls=%async_computation.4 | async-start | bytes 1048576 | tf_op jit(solution)/shard_map/all_to_all | solution.py:49
  324.6 33.5 %all-to-all-start.5 = ((bf16[32,2,256,16]{2,3,1,0:T(8,128)(2,1)}), bf16[32,2,256,16]{2,3,1,0:T(8,128)(2,1)S(1)}, u32[]{:S(2)}, u32[]{:S(2)}) async-start(bf16[32,2,256,16]{2,3,1,0:T(8,128)(2,1)} %copy.52), calls=%async_computation.5 | async-start | bytes 1048576 | tf_op jit(solution)/shard_map/all_to_all | solution.py:51
  358.2 2.6 copy-start.6
Sparse Core Ops, SparseCore 0:
  9.2 52.2 all-gather.1
where the time goes:
time: 370 us; the launch traced here: 369 us
  blocking collectives  219 us (59%)
  matrix products  61 us (16%)
  waiting for transfers between devices  39 us (11%)
  starting transfers between devices  22.1 us (6%)
  between operations  13.6 us (4%)
  local copies, waits for them, and re-layouts  10.1 us (3%)
    psum x2, blocking collectives, body(): cycle_partial = lax.psum(partial_value, 'col').astype(jnp.bfloat16)  169 us
    dot_general x32, matrix products, add_auxiliary(): jnp.einsum('pad,bd->pab', contracted, slab, preferred_element_type=jnp.fl...  54 us
    all_to_all x2, blocking collectives, body(): lax.all_to_all(cycle_term, 'row', split_axis=2, concat_axis=0, tiled=True)  50.7 us
    all_to_all x2, waiting for transfers between devices, body(): lax.all_to_all(first_move, 'col', split_axis=0, concat_axis=1, tiled=True)  29 us
    all_to_all x2, starting transfers between devices, body(): lax.all_to_all(flipped, 'row', split_axis=0, concat_axis=3, tiled=True)  13.1 us
    all_to_all x2, waiting for transfers between devices, body(): lax.all_to_all(flipped, 'row', split_axis=0, concat_axis=3, tiled=True)  9.26 us
    all_to_all x2, starting transfers between devices, body(): lax.all_to_all(first_move, 'col', split_axis=0, concat_axis=1, tiled=True)  8.97 us
  transfers between devices with their start and end apart: 5, of which 3 were waited for; matrix products, arithmetic and copies ran while one was open for 10% of the time, Pallas kernels for 0%

commit v1 on v0

v1 whole, which is shorter than its diff:
```python
import jax
import jax.numpy as jnp
from jax import lax
from jax.sharding import PartitionSpec as P

ITERS = 2


def body(amplitudes, coulomb, fit_ov, fit_vv, eps_occ, eps_vir):
    occ_local, occ_other, virtual, _ = amplitudes.shape
    n = lax.axis_size("row")
    occ_rows = lax.dynamic_slice_in_dim(eps_occ, lax.axis_index("row") * occ_local, occ_local)
    occ_cols = lax.dynamic_slice_in_dim(eps_occ, lax.axis_index("col") * occ_other, occ_other)
    denominator = (
        occ_rows[:, None, None, None]
        + occ_cols[None, :, None, None]
        - eps_vir[None, None, :, None]
        - eps_vir[None, None, None, :]
    )
    fitting = lax.all_gather(fit_vv, "row", axis=0, tiled=True)
    swap = [(r * n + c, c * n + r) for r in range(n) for c in range(n)]
    current = amplitudes
    for sweep in range(ITERS):
        partial_value = jnp.einsum(
            "qkc,ikac->qia", fit_ov, current, preferred_element_type=jnp.float32
        ).astype(jnp.bfloat16)
        piece = lax.psum_scatter(partial_value, "col", scatter_dimension=0, tiled=True)
        cycle_partial = lax.all_gather(piece, "col", axis=0, tiled=True)
        flat = current.reshape(occ_local * occ_other, virtual, virtual)
        contracted = jnp.einsum(
            "qac,pcd->paqd", fitting, flat, preferred_element_type=jnp.float32
        ).astype(jnp.bfloat16)
        ladder = jnp.einsum(
            "paqd,qbd->pab", contracted, fitting, preferred_element_type=jnp.float32
        ).reshape(occ_local, occ_other, virtual, virtual)
        cycle_term = jnp.einsum(
            "qia,qjb->ijab", cycle_partial, fit_ov, preferred_element_type=jnp.float32
        ).astype(jnp.bfloat16)
        moved = lax.ppermute(cycle_term, ("row", "col"), swap)
        returned = jnp.transpose(moved, (1, 0, 3, 2))
        summed = (
            coulomb.astype(jnp.float32)
            + ladder
            + cycle_term.astype(jnp.float32)
            + returned.astype(jnp.float32)
        )
        current = (summed / denominator).astype(jnp.bfloat16)
    return current


def solution(mesh):
    in_specs = (
        P("row", "col", None, None),
        P("row", "col", None, None),
        P(None, "col", None),
        P("row", None, None),
        P(),
        P(),
    )
    out_specs = P("row", "col", None, None)
    return jax.shard_map(body, mesh=mesh, in_specs=in_specs, out_specs=out_specs, check_vma=False)
```

time: 370 us -> 626 us (1.69)
  the two profiles are of different devices: /device:TPU:1 before, /device:TPU:7 now
where the time goes in v1:
time: 626 us; the launch traced here: 625 us
  waiting for transfers between devices  551 us (88%)
  matrix products  27.9 us (4%)
  starting transfers between devices  17.2 us (3%)
  between operations  15.4 us (2%)
  local copies, waits for them, and re-layouts  9.65 us (2%)
    reduce_scatter x1, waiting for transfers between devices, body(): lax.psum_scatter(partial_value, 'col', scatter_dimension=0, tiled=True)  199 us
    all_gather x2, waiting for transfers between devices, body(): cycle_partial = lax.all_gather(piece, 'col', axis=0, tiled=True)  151 us
    unnamed x6, waiting for transfers between devices  144 us
    ppermute x2, waiting for transfers between devices, body(): moved = lax.ppermute(cycle_term, ('row', 'col'), swap)  57.7 us
    dot_general x2, matrix products, body(): jnp.einsum('paqd,qbd->pab', contracted, fitting, preferred_element_type=j...  17.2 us
    ppermute x2, starting transfers between devices, body(): moved = lax.ppermute(cycle_term, ('row', 'col'), swap)  17.1 us
  transfers between devices with their start and end apart: 7, of which 6 were waited for; matrix products, arithmetic and copies ran while one was open for 3% of the time, Pallas kernels for 0%

profile of v1, /device:TPU:7, one launch (start us, length us, event | category | flops | bytes accessed | tf_op | source)
XLA Modules:
  0.0 625.0 jit_solution(13883543929066654249)
XLA Ops:
  7.4 0.0 copy-start
  7.4 0.0 reduce-scatter.2.cloned.1.call-start
  7.4 1.0 copy-done
  8.4 3.0 bitcast_convert_fusion.1
  11.4 0.0 reduce-scatter.2.cloned.1.call-update
  11.4 0.0 all-gather.4.cloned.1.call-start
  11.4 0.5 all-gather.4.cloned.1.call-update
  12.0 0.0 all-gather.6.cloned.1.call-start
  12.0 198.6 %reduce-scatter.2.cloned.1.call-done = bf16[64,2,256]{2,0,1:T(8,128)(2,1)} async-done(((bf16[1024,2,256]{2,0,1:T(8,128)(2,1)}), bf16[64,2,256]{2,0,1:T(8,128)(2,1)}) %reduce-scatter.2.cloned.1.call-update) | async-done | bytes 65552 | tf_op jit(solution)/shard_map/reduce_scatter | solution.py:27
  210.6 0.0 all-gather.6.cloned.1.call-update
  210.6 0.0 all-reduce.3.cloned.1.call-start
  210.7 0.0 all-gather.4.cloned.1.call-done
  210.7 0.0 copy-start.1
  210.7 0.0 copy-start.2
  210.7 9.2 %fusion.2 = f32[4,256,256,1]{2,1,3,0:T(8,128)} fusion(bf16[4,256,256,1]{2,1,3,0:T(8,128)(2,1)S(1)} %bitcast.77, bf16[16,256,256]{2,1,0:T(8,128)(2,1)} %all-gather.4.cloned.1.call-done), kind=kOutput, calls=%fused_computation.2 | convolution fusion | flops 4299161600 | bytes 3670016 | tf_op jit(solution)/shard_map/paqd,qbd->pab/dot_general | solution.py:33
  219.9 68.4 %all-gather.6.cloned.1.call-done = bf16[1024,2,256]{2,0,1:T(8,128)(2,1)} async-done(((bf16[64,2,256]{2,0,1:T(8,128)(2,1)}), bf16[1024,2,256]{2,0,1:T(8,128)(2,1)}) %all-gather.6.cloned.1.call-update) | async-done | bytes 1048592 | tf_op jit(solution)/shard_map/all_gather | solution.py:28
  288.3 0.0 copy-done.1
  288.3 0.0 copy-done.2
  288.3 0.0 copy-start.7
  288.3 0.0 copy-start.6
  288.3 3.1 fusion.17
  291.4 8.5 %collective-permute-start = (bf16[2,2,256,256]{3,2,1,0:T(8,128)(2,1)}, bf16[2,2,256,256]{3,2,1,0:T(8,128)(2,1)}, u32[]{:S(2)}, u32[]{:S(2)}) collective-permute-start(bf16[2,2,256,256]{3,2,1,0:T(8,128)(2,1)} %get-tuple-element.8), channel_id=1, source_target_pairs={{0,0},{1,16},{2,32},{3,48},{4,64},{5,80},{6,96},{7,112},{8,128},{9... | collective-permute-start | bytes 1572872 | tf_op jit(solution)/shard_map/ppermute | solution.py:39
  299.9 0.0 copy-done.7
  299.9 0.1 fusion.30
  300.0 0.1 broadcast_add_fusion
  300.1 0.0 copy-done.6
  300.1 0.1 broadcast_subtract_fusion
  300.1 0.3 copy.36
  300.5 0.0 copy-start.3
  300.5 33.5 %collective-permute-done = bf16[2,2,256,256]{3,2,1,0:T(8,128)(2,1)} collective-permute-done((bf16[2,2,256,256]{3,2,1,0:T(8,128)(2,1)}, bf16[2,2,256,256]{3,2,1,0:T(8,128)(2,1)}, u32[]{:S(2)}, u32[]{:S(2)}) %collective-permute-start) | collective-permute-done | bytes 524320 | tf_op jit(solution)/shard_map/ppermute | solution.py:39
  334.0 1.3 fusion.19
  335.3 0.0 copy-done.3
  335.3 1.8 fusion.14
  337.0 0.0 copy-start.8
  337.0 0.0 copy-start.4
  337.1 3.7 copy.42
  340.8 0.0 all-reduce.3.cloned.1.call-update
  340.8 0.0 all-gather.8.cloned.1.call-start
  340.9 0.0 copy-done.8
  340.9 0.6 dynamic-slice
  342.1 143.1 %all-reduce.3.cloned.1.call-done = bf16[1024,2,256]{2,1,0:T(2,128)(2,1)} async-done(((bf16[1024,2,256]{2,1,0:T(2,128)(2,1)}), bf16[1024,2,256]{2,1,0:T(2,128)(2,1)}) %all-reduce.3.cloned.1.call-update) | async-done | bytes 1048592
  485.2 1.5 constant_dynamic-slice_fusion
  486.7 0.0 all-gather.8.cloned.1.call-update
  486.7 1.0 copy.37
  487.7 82.7 %all-gather.8.cloned.1.call-done = bf16[1024,2,256]{2,1,0:T(2,128)(2,1)} async-done(((bf16[64,2,256]{2,1,0:T(2,128)(2,1)}), bf16[1024,2,256]{2,1,0:T(2,128)(2,1)}) %all-gather.8.cloned.1.call-update) | async-done | bytes 1048592 | tf_op jit(solution)/shard_map/all_gather | solution.py:28
  570.4 0.0 copy-done.4
  570.4 0.0 copy-start.5
  570.4 2.8 fusion.16
  573.2 8.6 %collective-permute-start.1 = (bf16[2,2,256,256]{3,2,1,0:T(8,128)(2,1)}, bf16[2,2,256,256]{3,2,1,0:T(8,128)(2,1)}, u32[]{:S(2)}, u32[]{:S(2)}) collective-permute-start(bf16[2,2,256,256]{3,2,1,0:T(8,128)(2,1)} %fusion.16), channel_id=1, source_target_pairs={{0,0},{1,16},{2,32},{3,48},{4,64},{5,80},{6,96},{7,112},{8,128},{9... | collective-permute-start | bytes 1572872 | tf_op jit(solution)/shard_map/ppermute | solution.py:39
  581.8 0.0 copy-done.5
  581.8 8.1 %fusion = f32[4,256,256,1]{2,1,3,0:T(8,128)S(1)} fusion(bf16[4,256,256,1]{2,1,3,0:T(8,128)(2,1)S(1)} %bitcast.81, bf16[16,256,256]{2,1,0:T(8,128)(2,1)} %all-gather.4.cloned.1.call-done), kind=kOutput, calls=%fused_computation | convolution fusion | flops 4299161600 | bytes 3670016 | tf_op jit(solution)/shard_map/paqd,qbd->pab/dot_general | solution.py:33
  589.9 1.2 fusion.18
  591.1 0.3 copy.45
  591.4 24.2 %collective-permute-done.1 = bf16[2,2,256,256]{3,2,1,0:T(8,128)(2,1)} collective-permute-done((bf16[2,2,256,256]{3,2,1,0:T(8,128)(2,1)}, bf16[2,2,256,256]{3,2,1,0:T(8,128)(2,1)}, u32[]{:S(2)}, u32[]{:S(2)}) %collective-permute-start.1) | collective-permute-done | bytes 524320 | tf_op jit(solution)/shard_map/ppermute | solution.py:39
  615.6 1.3 fusion.20
  616.9 1.0 copy.46
Async XLA Ops:
  7.4 1.0 copy-start
  7.4 203.2 %reduce-scatter.2.cloned.1.call-start = ((), (), s32[]{:S(2)}) async-start(), calls=%async_computation.2 | async-start | bytes 1114112 | tf_op jit(solution)/shard_map/reduce_scatter | solution.py:27
  11.4 199.3 %all-gather.4.cloned.1.call-start = ((), (), s32[]{:S(2)}) async-start(), calls=%async_computation.1 | async-start | bytes 2228224 | tf_op jit(solution)/shard_map/all_gather | solution.py:20
  12.0 276.3 %all-gather.6.cloned.1.call-start = ((), (), s32[]{:S(2)}) async-start(), calls=%async_computation.3 | async-start | bytes 1114112 | tf_op jit(solution)/shard_map/all_gather | solution.py:28
  210.6 274.6 %all-reduce.3.cloned.1.call-start = ((), (), s32[]{:S(2)}) async-start(), calls=%async_computation.5 | async-start | bytes 2097152
  210.7 77.6 %copy-start.1 = (bf16[2,2,256,256]{3,2,1,0:T(8,128)(2,1)S(1)}, bf16[2,2,256,256]{3,2,1,0:T(8,128)(2,1)}, u32[]{:S(2)}) copy-start(bf16[2,2,256,256]{3,2,1,0:T(8,128)(2,1)} %param.7) | copy-start | bytes 1572868
  210.7 77.6 %copy-start.2 = (bf16[1024,2,256]{2,1,0:T(2,128)(2,1)S(1)}, bf16[1024,2,256]{2,1,0:T(2,128)(2,1)}, u32[]{:S(2)}) copy-start(bf16[1024,2,256]{2,1,0:T(2,128)(2,1)} %param.8) | copy-start | bytes 3145732
  288.3 11.6 %copy-start.7 = (f32[32]{0:T(128)S(1)}, f32[32]{0:T(128)}, u32[]{:S(2)}) copy-start(f32[32]{0:T(128)} %param.10) | copy-start | bytes 388
  288.3 11.8 %copy-start.6 = (f32[256]{0:T(256)S(1)}, f32[256]{0:T(256)}, u32[]{:S(2)}) copy-start(f32[256]{0:T(256)} %param.11) | copy-start | bytes 3076
  291.4 42.6 %collective-permute-start = (bf16[2,2,256,256]{3,2,1,0:T(8,128)(2,1)}, bf16[2,2,256,256]{3,2,1,0:T(8,128)(2,1)}, u32[]{:S(2)}, u32[]{:S(2)}) collective-permute-start(bf16[2,2,256,256]{3,2,1,0:T(8,128)(2,1)} %get-tuple-element.8), channel_id=1, source_target_pairs={{0,0},{1,16},{2,32},{3,48},{4,64},{5,80},{6,96},{7,112},{8,128},{9... | collective-permute-start | bytes 1572872 | tf_op jit(solution)/shard_map/ppermute | solution.py:39
  300.5 34.8 %copy-start.3 = (bf16[1024,2,256]{2,1,0:T(2,128)(2,1)S(1)}, bf16[1024,2,256]{2,1,0:T(2,128)(2,1)}, u32[]{:S(2)}) copy-start(bf16[1024,2,256]{2,1,0:T(2,128)(2,1)} %param.8) | copy-start | bytes 3145732
  337.0 3.8 copy-start.8
  337.0 233.3 %copy-start.4 = (bf16[1024,2,256]{2,1,0:T(2,128)(2,1)S(1)}, bf16[1024,2,256]{2,1,0:T(2,128)(2,1)}, u32[]{:S(2)}) copy-start(bf16[1024,2,256]{2,1,0:T(2,128)(2,1)} %param.8) | copy-start | bytes 3145732
  340.8 229.6 %all-gather.8.cloned.1.call-start = ((), (), s32[]{:S(2)}) async-start(), calls=%async_computation.4 | async-start | bytes 1114112 | tf_op jit(solution)/shard_map/all_gather | solution.py:28
  570.4 11.4 %copy-start.5 = (bf16[2,2,256,256]{3,2,1,0:T(8,128)(2,1)S(1)}, bf16[2,2,256,256]{3,2,1,0:T(8,128)(2,1)}, u32[]{:S(2)}) copy-start(bf16[2,2,256,256]{3,2,1,0:T(8,128)(2,1)} %copy.37) | copy-start | bytes 1572868
  573.2 42.4 %collective-permute-start.1 = (bf16[2,2,256,256]{3,2,1,0:T(8,128)(2,1)}, bf16[2,2,256,256]{3,2,1,0:T(8,128)(2,1)}, u32[]{:S(2)}, u32[]{:S(2)}) collective-permute-start(bf16[2,2,256,256]{3,2,1,0:T(8,128)(2,1)} %fusion.16), channel_id=1, source_target_pairs={{0,0},{1,16},{2,32},{3,48},{4,64},{5,80},{6,96},{7,112},{8,128},{9... | collective-permute-start | bytes 1572872 | tf_op jit(solution)/shard_map/ppermute | solution.py:39
Sparse Core Ops, SparseCore 0:
  12.0 198.5 reduce-scatter.1
  340.9 144.1 all-reduce.2
  487.8 82.5 all-gather.7
Sparse Core Ops, SparseCore 1:
  13.7 38.6 all-gather.3
  210.7 77.5 all-gather.5

commit v2 on v1

v2 whole, which is shorter than its diff:
```python
import jax
import jax.numpy as jnp
from jax import lax
from jax.experimental import pallas as pl
from jax.experimental.pallas import tpu as pltpu
from jax.sharding import PartitionSpec as P

ITERS = 2
MESH = pl.DeviceIdType.MESH
F32 = jnp.float32
BF16 = jnp.bfloat16

ZN = 8
XN = 4
RIGHT, LEFT = 0, 1
SUBS = 4
FP = 8


def nn(a, b):
    return jnp.dot(a, b, preferred_element_type=F32)


def nt(a, b):
    return lax.dot_general(a, b, (((1,), (1,)), ((), ())), preferred_element_type=F32)


def tt(a, b):
    return lax.dot_general(a, b, (((0,), (1,)), ((), ())), preferred_element_type=F32)


def kernel(occ, amp, coul, fit, own_b, ev_row, ev_col, out,
           t2, part, rs, yv, yr, pp, fr, bs, acc, con,
           rs_sem, y_sem, ag_sem, bc_sem, f_sem, b_sem,
           rs_send, y_send, ag_send, bc_send, f_send, b_send, local_sem):
    row = lax.axis_index("row")
    col = lax.axis_index("col")
    core = lax.rem(row, 2)
    x = lax.rem(row // 2, XN)
    yl = row // (2 * XN)
    z = lax.rem(col, ZN)
    yh = col // ZN

    def dev(yl_, x_, core_, yh_, z_):
        return (yl_ * (2 * XN) + x_ * 2 + core_, yh_ * ZN + z_)

    z_next = dev(yl, x, core, yh, lax.rem(z + 1, ZN))
    z_prev = dev(yl, x, core, yh, lax.rem(z + ZN - 1, ZN))
    x_next = dev(yl, lax.rem(x + 1, XN), core, yh, z)
    x_prev = dev(yl, lax.rem(x + XN - 1, XN), core, yh, z)
    y_far = dev(yl, x, core, 1 - yh, z)
    y_near = dev(1 - yl, x, core, yh, z)
    y_both = dev(1 - yl, x, core, 1 - yh, z)
    mate = dev(yl, x, 1 - core, yh, z)

    barrier = pltpu.get_barrier_semaphore()
    for peer in (z_next, z_prev, x_next, x_prev, y_far, y_near, y_both, mate):
        pl.semaphore_signal(barrier, inc=1, device_id=peer, device_id_type=MESH)
    pl.semaphore_wait(barrier, 8)

    def send(src, dst, send_sem, recv_sem, peer):
        pltpu.make_async_remote_copy(
            src_ref=src, dst_ref=dst, send_sem=send_sem, recv_sem=recv_sem,
            device_id=peer, device_id_type=MESH,
        ).start()

    def arrived(ref, sem):
        pltpu.make_async_copy(ref, ref, sem).wait()

    chunk = part.shape[1] // ZN
    sub = chunk // SUBS
    half = chunk // 2
    virtual = amp.shape[2]
    f_rows = fit.shape[0] // (2 * FP)
    ring = {RIGHT: z_next, LEFT: z_prev}

    def rows_of(o, s):
        return pl.ds(pl.multiple_of(o * chunk + s * sub, sub), sub)

    z_seed = 2 * x + core
    far_plane = (yl != yh).astype(jnp.int32)
    d_right = lax.rem(z + ZN - z_seed, ZN)
    d_left = lax.rem(z_seed + ZN - z, ZN)
    is_seed = z == z_seed

    def f_ref(ref, way, p):
        return ref.at[pl.ds(pl.multiple_of((way * FP + p) * f_rows, f_rows), f_rows)]

    @pl.when(jnp.logical_and(is_seed, far_plane == 0))
    def _():
        own = pltpu.make_async_copy(fit, fr, local_sem)
        own.start()
        own.wait()

    @pl.when(jnp.logical_and(is_seed, far_plane == 1))
    def _():
        for way in (RIGHT, LEFT):
            for p in range(FP):
                send(f_ref(fit, way, p), f_ref(fr, way, p), f_send.at[2], f_sem.at[way, p], y_both)

    def f_step(k):
        for way, d in ((RIGHT, d_right), (LEFT, d_left)):
            p = k - d - far_plane

            @pl.when(jnp.logical_and(p >= 0, p < FP))
            def _(way=way, d=d, p=p):
                ref = f_ref(fr, way, p)

                @pl.when(jnp.logical_or(d > 0, far_plane == 1))
                def _():
                    arrived(ref, f_sem.at[way, p])

                @pl.when(d < ZN - 1)
                def _():
                    send(ref, ref, f_send.at[way], f_sem.at[way, p], ring[way])

    def pair(x_):
        return bs.at[pl.ds(core * 8 + x_ * 2, 2)]

    def block(x_, yl_):
        return bs.at[pl.ds(core * 8 + x_ * 2 + yl_, 1)]

    x_up = lax.rem(x + 1, XN)
    x_down = lax.rem(x + XN - 1, XN)
    x_two = lax.rem(x + 2, XN)

    def b_step(k):
        @pl.when(k == 0)
        def _():
            send(own_b, block(x, yl), b_send.at[0], b_sem.at[0], y_near)
            own = pltpu.make_async_copy(own_b, block(x, yl), local_sem)
            own.start()
            own.wait()

        @pl.when(k == 1)
        def _():
            arrived(block(x, 1 - yl), b_sem.at[0])
            send(pair(x), pair(x), b_send.at[1], b_sem.at[1], x_next)
            send(pair(x), pair(x), b_send.at[2], b_sem.at[2], x_prev)

        @pl.when(k == 2)
        def _():
            arrived(pair(x_down), b_sem.at[1])
            arrived(pair(x_up), b_sem.at[2])
            send(block(x_down, yl), block(x_down, yl), b_send.at[3], b_sem.at[3], x_next)
            send(block(x_up, 1 - yl), block(x_up, 1 - yl), b_send.at[4], b_sem.at[4], x_prev)

        @pl.when(k == 3)
        def _():
            arrived(block(x_two, yl), b_sem.at[3])
            arrived(block(x_two, 1 - yl), b_sem.at[4])
            lane = bs.at[pl.ds(core * 8, 8)]
            send(lane, lane, b_send.at[5], b_sem.at[5], mate)

    dx = lax.rem(x + XN - z // 2, XN)
    on_lane = core == lax.rem(z, 2)
    on_plane = jnp.logical_and(on_lane, yl == yh)
    is_src = jnp.logical_and(on_plane, dx == 0)
    sel = 1 - is_src.astype(jnp.int32)
    depth = (
        jnp.where(dx == 2, 2, jnp.where(dx == 0, 0, 1))
        + (yl != yh).astype(jnp.int32)
        + jnp.logical_not(on_lane).astype(jnp.int32)
    )

    for i in range(2):
        for j in range(2):
            t2[i * virtual:(i + 1) * virtual, j * virtual:(j + 1) * virtual] = amp[i, j]

    @pl.loop(0, ITERS)
    def _(it):
        first = it == 0

        for m in range(2):
            part[it, m * virtual:(m + 1) * virtual, :] = nt(
                t2[m * virtual:(m + 1) * virtual, :], fit[...]
            ).astype(BF16)
        acc[...] = jnp.zeros_like(acc)

        @pl.loop(0, 4)
        def _(h):
            for s in range(SUBS):
                for way, o, late in (
                    (RIGHT, lax.rem(z + 4 - h, ZN), int(s >= 2)),
                    (LEFT, lax.rem(z + 4 + h, ZN), int(s < 2)),
                ):
                    @pl.when(h >= late)
                    def _(way=way, o=o, late=late, s=s):
                        at = rows_of(o, s)
                        where = pl.ds(s * sub, sub)

                        @pl.when(h > late)
                        def _():
                            slot = rs.at[it, way, h - 1, where]
                            arrived(slot, rs_sem.at[it, way, h - 1, s])
                            part[it, at, :] = (part[it, at, :].astype(F32) + slot[...].astype(F32)).astype(BF16)

                        send(part.at[it, at], rs.at[it, way, h, where], rs_send.at[it],
                             rs_sem.at[it, way, h, s], ring[way])

            @pl.when(first)
            def _():
                f_step(h)
                b_step(h)

        for s in range(SUBS):
            at = rows_of(z, s)
            where = pl.ds(s * sub, sub)
            for way in (RIGHT, LEFT):
                arrived(rs.at[it, way, 3, where], rs_sem.at[it, way, 3, s])
            yv[it, where, :] = (
                part[it, at, :].astype(F32)
                + rs[it, RIGHT, 3, where, :].astype(F32)
                + rs[it, LEFT, 3, where, :].astype(F32)
            ).astype(BF16)
            send(yv.at[it, where], yr.at[it, where], y_send.at[it], y_sem.at[it, s], y_far)
        for s in range(SUBS):
            at = rows_of(z, s)
            where = pl.ds(s * sub, sub)
            arrived(yr.at[it, where], y_sem.at[it, s])
            pp[it, 0, at, :] = (yv[it, where, :].astype(F32) + yr[it, where, :].astype(F32)).astype(BF16)
            for way in (RIGHT, LEFT):
                send(pp.at[it, 0, at], pp.at[it, 0, at], ag_send.at[it], ag_sem.at[it, way, 0, s], ring[way])

        @pl.loop(0, 9)
        def _(n):
            @pl.when(jnp.logical_and(n >= 1, n <= 4))
            def _():
                for s in range(SUBS):
                    for way, o, most in (
                        (RIGHT, lax.rem(z + ZN - n, ZN), 4 if s < 2 else 3),
                        (LEFT, lax.rem(z + n, ZN), 4 if s >= 2 else 3),
                    ):
                        @pl.when(n <= most)
                        def _(way=way, o=o, most=most, s=s):
                            at = rows_of(o, s)
                            ref = pp.at[it, 0, at]
                            arrived(ref, ag_sem.at[it, way, n - 1, s])

                            @pl.when(n < most)
                            def _():
                                send(ref, ref, ag_send.at[it], ag_sem.at[it, way, n, s], ring[way])

            m = n - depth

            @pl.when(jnp.logical_and(m >= 0, m <= 4))
            def _():
                for hf in range(2):
                    for sign in (0, 1):
                        o = lax.rem(z + ZN - m, ZN) if sign == 0 else lax.rem(z + m, ZN)
                        used = True if sign == 0 else jnp.logical_and(m >= 1, m <= 3)

                        @pl.when(used)
                        def _(o=o, hf=hf):
                            at = pl.ds(pl.multiple_of(o * chunk + hf * half, half), half)
                            src = pp.at[it, sel, at]
                            dst = pp.at[it, 1, at]
                            sem = bc_sem.at[it, o * 2 + hf]

                            @pl.when(sel == 1)
                            def _():
                                arrived(dst, sem)

                            @pl.when(jnp.logical_and(on_plane, jnp.logical_or(dx == 0, (dx == 1) if hf == 0 else False)))
                            def _():
                                send(src, dst, bc_send.at[it, 0], sem, x_next)

                            @pl.when(jnp.logical_and(on_plane, jnp.logical_or(dx == 0, (dx == 3) if hf == 1 else False)))
                            def _():
                                send(src, dst, bc_send.at[it, 1], sem, x_prev)

                            @pl.when(on_plane)
                            def _():
                                send(src, dst, bc_send.at[it, 2], sem, y_near)

                            @pl.when(on_lane)
                            def _():
                                send(src, dst, bc_send.at[it, 3], sem, mate)

            @pl.when(first)
            def _():
                f_step(n + 4)

                @pl.when(n == 2)
                def _():
                    other = bs.at[pl.ds((1 - core) * 8, 8)]
                    arrived(other, b_sem.at[5])

            @pl.when(n < 4)
            def _():
                start = lax.rem(core * 8 + n * 4, 16)
                bb = bs[pl.ds(start, 4)].reshape(4 * virtual, virtual)
                for p in range(4):
                    i, j = p // 2, p % 2
                    con[p] = nn(
                        bb, t2[i * virtual:(i + 1) * virtual, j * virtual:(j + 1) * virtual]
                    ).astype(BF16)
                for p in range(4):
                    total = acc[p]
                    for k in range(4):
                        total = total + nt(con[p, k * virtual:(k + 1) * virtual, :], bb[k * virtual:(k + 1) * virtual])
                    acc[p] = total

            @pl.when(jnp.logical_and(n >= 5, n < 7))
            def _():
                i = n - 5
                term = nn(pp[it, 0, pl.ds(pl.multiple_of(i * virtual, virtual), virtual), :], fit[...])
                for j in range(2):
                    acc[2 * i + j] += term[:, j * virtual:(j + 1) * virtual]

        @pl.when(first)
        def _():
            @pl.loop(13, 16)
            def _(k):
                f_step(k)

        for i in range(2):
            term = tt(fr[:, i * virtual:(i + 1) * virtual], pp[it, sel])
            for j in range(2):
                total = coul[i, j].astype(F32) + acc[2 * i + j] + term[:, j * virtual:(j + 1) * virtual]
                denominator = occ[i, j] - ev_col[...] - ev_row[...]
                updated = (total / denominator).astype(BF16)
                t2[i * virtual:(i + 1) * virtual, j * virtual:(j + 1) * virtual] = updated
                out[i, j] = updated

        sent = part.at[it, pl.ds(0, 7 * chunk)]
        arrived(sent, rs_send.at[it])
        arrived(sent, ag_send.at[it])
        arrived(yv.at[it], y_send.at[it])
        whole = pp.at[it, 0]
        fewer = pp.at[it, 0, pl.ds(0, 4 * chunk)]
        for way, near in ((0, 1), (1, 3)):
            @pl.when(is_src)
            def _(way=way):
                arrived(whole, bc_send.at[it, way])

            @pl.when(jnp.logical_and(on_plane, dx == near))
            def _(way=way):
                arrived(fewer, bc_send.at[it, way])

        @pl.when(on_plane)
        def _():
            arrived(whole, bc_send.at[it, 2])

        @pl.when(on_lane)
        def _():
            arrived(whole, bc_send.at[it, 3])

    f_half = fr.at[pl.ds(0, FP * f_rows)]
    for way, d in ((RIGHT, d_right), (LEFT, d_left)):
        @pl.when(d < ZN - 1)
        def _(way=way):
            arrived(f_half, f_send.at[way])

    @pl.when(jnp.logical_and(is_seed, far_plane == 1))
    def _():
        arrived(fr, f_send.at[2])

    arrived(block(x, yl), b_send.at[0])
    arrived(pair(x), b_send.at[1])
    arrived(pair(x), b_send.at[2])
    arrived(block(x, yl), b_send.at[3])
    arrived(block(x, yl), b_send.at[4])
    arrived(bs.at[pl.ds(core * 8, 8)], b_send.at[5])


def body(amplitudes, coulomb, fit_ov, fit_vv, eps_occ, eps_vir):
    occ_local, occ_other, virtual, _ = amplitudes.shape
    aux = fit_ov.shape[0]
    side = occ_local * virtual
    chunk = side // ZN
    occ_rows = lax.dynamic_slice_in_dim(eps_occ, lax.axis_index("row") * occ_local, occ_local)
    occ_cols = lax.dynamic_slice_in_dim(eps_occ, lax.axis_index("col") * occ_other, occ_other)
    occ = occ_rows[:, None] + occ_cols[None, :]
    fit = fit_ov.reshape(aux, occ_other * virtual)
    batch = fit_vv.shape[0] * lax.axis_size("row")
    vmem = pl.BlockSpec(memory_space=pltpu.VMEM)
    dma = pltpu.SemaphoreType.DMA
    return pl.pallas_call(
        kernel,
        out_shape=jax.ShapeDtypeStruct(amplitudes.shape, BF16),
        in_specs=[pl.BlockSpec(memory_space=pltpu.SMEM)] + [vmem] * 6,
        out_specs=vmem,
        scratch_shapes=[
            pltpu.VMEM((side, occ_other * virtual), BF16),
            pltpu.VMEM((ITERS, side, aux), BF16),
            pltpu.VMEM((ITERS, 2, 4, chunk, aux), BF16),
            pltpu.VMEM((ITERS, chunk, aux), BF16),
            pltpu.VMEM((ITERS, chunk, aux), BF16),
            pltpu.VMEM((ITERS, 2, side, aux), BF16),
            pltpu.VMEM((aux, side), BF16),
            pltpu.VMEM((batch, virtual, virtual), BF16),
            pltpu.VMEM((occ_local * occ_other, virtual, virtual), F32),
            pltpu.VMEM((4, 4 * virtual, virtual), BF16),
            dma((ITERS, 2, 4, SUBS)),
            dma((ITERS, SUBS)),
            dma((ITERS, 2, 4, SUBS)),
            dma((ITERS, 2 * ZN)),
            dma((2, FP)),
            dma((6,)),
            dma((ITERS,)),
            dma((ITERS,)),
            dma((ITERS,)),
            dma((ITERS, 4)),
            dma((3,)),
            dma((6,)),
            dma,
        ],
        compiler_params=pltpu.CompilerParams(
            collective_id=0, has_side_effects=True, vmem_limit_bytes=60 * 2**20
        ),
        name="sweeps",
    )(occ, amplitudes, coulomb, fit, fit_vv, eps_vir[None, :], eps_vir[:, None])


def solution(mesh):
    in_specs = (
        P("row", "col", None, None),
        P("row", "col", None, None),
        P(None, "col", None),
        P("row", None, None),
        P(),
        P(),
    )
    out_specs = P("row", "col", None, None)
    return jax.shard_map(body, mesh=mesh, in_specs=in_specs, out_specs=out_specs, check_vma=False)
```

time: 626 us -> 133 us (0.21)
  the two profiles are of different devices: /device:TPU:7 before, /device:TPU:13 now
where the time goes in v2:
time: 133 us
  Pallas kernels  126 us (95%)
  local copies, waits for them, and re-layouts  5.85 us (4%)
    pallas_call x1, Pallas kernels, body(): pl.pallas_call(kernel, out_shape=jax.ShapeDtypeStruct(amplitudes.shape, B...  126 us
    unnamed x6, local copies, waits for them, and re-layouts  4.98 us

profile of v2, /device:TPU:13, one launch (start us, length us, event | category | flops | bytes accessed | tf_op | source)
XLA Modules:
  0.0 132.9 jit_solution(4637516808595785811)
XLA Ops:
  0.0 0.0 copy-start.1
  0.0 0.7 copy-done.1
  0.7 0.1 fusion
  0.7 0.0 copy-start
  0.7 0.6 broadcast_add_fusion.occ
  1.4 0.0 copy-done
  1.4 0.8 copy.7.ev_col
  2.2 2.4 %copy.8 = bf16[128,8,2,256]{3,1,2,0:T(8,128)(2,1)} copy(bf16[128,8,2,256]{3,2,1,0:T(2,128)(2,1)} %bitcast.5) | data formatting | bytes 2097152
  4.6 126.4 %sweeps.1 = bf16[2,2,256,256]{3,2,1,0:T(8,128)(2,1)} custom-call(f32[2,2]{1,0:T(2,128)} %broadcast_add_fusion.occ, bf16[2,2,256,256]{3,2,1,0:T(8,128)(2,1)} %amp.1, bf16[2,2,256,256]{3,2,1,0:T(8,128)(2,1)} %coul.1, bf16[1024,512]{1,0:T(8,128)(2,1)} %bitcast.4, bf16[1,256,256]{2,1,0:T(8,128)(2,1)} %own_b.1, f32[1,256]{1,0:T(1,128)} %bitcast.6, ...), custom_call_target="tpu_custom_call" | custom-call | tf_op jit(solution)/shard_map/sweeps/pallas_call | solution.py:379
  131.0 1.9 %copy.10 = bf16[2,2,256,256]{3,2,1,0:T(8,128)(2,1)} copy(bf16[2,2,256,256]{3,2,1,0:T(8,128)(2,1)} %sweeps.1) | data formatting | bytes 1048576
Async XLA Ops:
  0.0 0.7 copy-start.1
  0.7 0.7 copy-start

commit v3 on v2

v3 whole, which is shorter than its diff:
```python
import jax
import jax.numpy as jnp
from jax import lax
from jax.experimental import pallas as pl
from jax.experimental.pallas import tpu as pltpu
from jax.sharding import PartitionSpec as P

ITERS = 2
MESH = pl.DeviceIdType.MESH
F32 = jnp.float32
BF16 = jnp.bfloat16

ZN = 8
XN = 4
RIGHT, LEFT = 0, 1
F_OVER = 9
FP = 4


def nn(a, b):
    return jnp.dot(a, b, preferred_element_type=F32)


def nt(a, b):
    return lax.dot_general(a, b, (((1,), (1,)), ((), ())), preferred_element_type=F32)


def tt(a, b):
    return lax.dot_general(a, b, (((0,), (1,)), ((), ())), preferred_element_type=F32)


def kernel(eps, amp, coul, fit, own_b, ev_row, out,
           t2, part, rsa, rsb, yfirst, yv, yr, pp, fr, bs, acc, con, ev_col,
           rsa_sem, rsb_sem, y_sem, aga_sem, agb_sem, bc_sem, f_sem, b_sem,
           rs_send, y_send, ag_send, bc_send, f_send, b_send, local_sem):
    row = lax.axis_index("row")
    col = lax.axis_index("col")
    core = lax.rem(row, 2)
    x = lax.rem(row // 2, XN)
    yl = row // (2 * XN)
    z = lax.rem(col, ZN)
    yh = col // ZN

    def dev(yl_, x_, core_, yh_, z_):
        return (yl_ * (2 * XN) + x_ * 2 + core_, yh_ * ZN + z_)

    z_next = dev(yl, x, core, yh, lax.rem(z + 1, ZN))
    z_prev = dev(yl, x, core, yh, lax.rem(z + ZN - 1, ZN))
    x_next = dev(yl, lax.rem(x + 1, XN), core, yh, z)
    x_prev = dev(yl, lax.rem(x + XN - 1, XN), core, yh, z)
    y_far = dev(yl, x, core, 1 - yh, z)
    y_near = dev(1 - yl, x, core, yh, z)
    y_both = dev(1 - yl, x, core, 1 - yh, z)
    mate = dev(yl, x, 1 - core, yh, z)

    z_next2 = dev(yl, x, core, yh, lax.rem(z + 2, ZN))
    z_prev2 = dev(yl, x, core, yh, lax.rem(z + ZN - 2, ZN))
    near_mate = dev(1 - yl, x, 1 - core, yh, z)
    far_plane = (yl != yh).astype(jnp.int32)

    def plane_peer(flip, shift):
        yl_ = jnp.where(flip == 1, 1 - yl, yl)
        yh_ = jnp.where(flip == 1, 1 - yh, yh)
        return dev(yl_, lax.rem(x + shift, XN), core, yh_, z)

    barrier = pltpu.get_barrier_semaphore()
    peers = [z_next, z_prev, z_next2, z_prev2, y_far, y_near, near_mate, mate]
    peers += [plane_peer(0, shift) for shift in range(1, XN)] + [plane_peer(1, shift) for shift in range(XN)]
    for peer in peers:
        pl.semaphore_signal(barrier, inc=1, device_id=peer, device_id_type=MESH)
    pl.semaphore_wait(barrier, len(peers))

    def send(src, dst, send_sem, recv_sem, peer):
        pltpu.make_async_remote_copy(
            src_ref=src, dst_ref=dst, send_sem=send_sem, recv_sem=recv_sem,
            device_id=peer, device_id_type=MESH,
        ).start()

    def arrived(ref, sem):
        pltpu.make_async_copy(ref, ref, sem).wait()

    virtual = amp.shape[2]
    side = part.shape[1]
    sub = side // (4 * ZN)
    f_rows = fit.shape[0] // (4 * FP)
    ring = {RIGHT: z_next, LEFT: z_prev}
    ring2 = {RIGHT: z_next2, LEFT: z_prev2}
    toward = {RIGHT: 1, LEFT: ZN - 1}
    even = lax.rem(z, 2) == 0
    b_long = {RIGHT: even, LEFT: jnp.logical_not(even)}

    def a_rows(o, s):
        return pl.ds(pl.multiple_of((o * 2 + s) * sub, sub), sub)

    def b_rows(v, o):
        return pl.ds(pl.multiple_of(side // 2 + v * (side // 4) + o * sub, sub), sub)

    z_seed = 2 * x + core
    d_right = lax.rem(z + ZN - z_seed, ZN)
    d_left = lax.rem(z_seed + ZN - z, ZN)
    is_seed = z == z_seed

    def f_ref(ref, v, way, p):
        return ref.at[pl.ds(pl.multiple_of(((v * 2 + way) * FP + p) * f_rows, f_rows), f_rows)]

    @pl.when(jnp.logical_and(is_seed, far_plane == 0))
    def _():
        ref = pl.ds(pl.multiple_of(yh * 2 * FP * f_rows, f_rows), 2 * FP * f_rows)
        own = pltpu.make_async_copy(fit.at[ref], fr.at[ref], local_sem)
        own.start()
        own.wait()

    def f_seed():
        @pl.when(jnp.logical_and(is_seed, far_plane == 1))
        def _():
            for p in range(FP):
                for way in (RIGHT, LEFT):
                    send(f_ref(fit, 1 - yh, way, p), f_ref(fr, 1 - yh, way, p), f_send.at[2], f_sem.at[0, way, p], y_both)

    def f_delay(d):
        return 2 * d + 2 * far_plane

    def f_over(k):
        for p in range(FP):
            for way, d in ((RIGHT, d_right), (LEFT, d_left)):
                @pl.when(k == jnp.maximum(p + f_delay(d), F_OVER))
                def _(way=way, p=p):
                    ref = f_ref(fr, yh, way, p)
                    send(ref, ref, f_send.at[3], f_sem.at[1, way, p], y_far)

    def f_step(k):
        for way, d in ((RIGHT, d_right), (LEFT, d_left)):
            p = k - f_delay(d)

            @pl.when(jnp.logical_and(p >= 0, p < FP))
            def _(way=way, d=d, p=p):
                ref = f_ref(fr, yh, way, p)

                @pl.when(jnp.logical_or(d > 0, far_plane == 1))
                def _():
                    arrived(ref, f_sem.at[0, way, p])

                @pl.when(d < ZN - 1)
                def _():
                    send(ref, ref, f_send.at[way], f_sem.at[0, way, p], ring[way])

    def pair(x_):
        return bs.at[pl.ds(core * 8 + x_ * 2, 2)]

    def block(x_, yl_):
        return bs.at[pl.ds(core * 8 + x_ * 2 + yl_, 1)]

    x_up = lax.rem(x + 1, XN)
    x_down = lax.rem(x + XN - 1, XN)
    x_two = lax.rem(x + 2, XN)

    def b_step(k):
        @pl.when(k == 0)
        def _():
            send(own_b, block(x, yl), b_send.at[0], b_sem.at[0], y_near)
            own = pltpu.make_async_copy(own_b, block(x, yl), local_sem)
            own.start()
            own.wait()

        @pl.when(k == 2)
        def _():
            arrived(block(x, 1 - yl), b_sem.at[0])
            send(pair(x), pair(x), b_send.at[1], b_sem.at[1], x_next)
            send(pair(x), pair(x), b_send.at[2], b_sem.at[2], x_prev)

        @pl.when(k == 4)
        def _():
            arrived(pair(x_down), b_sem.at[1])
            arrived(pair(x_up), b_sem.at[2])
            send(block(x_down, yl), block(x_down, yl), b_send.at[3], b_sem.at[3], x_next)
            send(block(x_up, 1 - yl), block(x_up, 1 - yl), b_send.at[4], b_sem.at[4], x_prev)

        @pl.when(k == 6)
        def _():
            arrived(block(x_two, yl), b_sem.at[3])
            arrived(block(x_two, 1 - yl), b_sem.at[4])
            lane = bs.at[pl.ds(core * 8, 8)]
            send(lane, lane, b_send.at[5], b_sem.at[5], mate)

        @pl.when(k == 8)
        def _():
            other = bs.at[pl.ds((1 - core) * 8, 8)]
            arrived(other, b_sem.at[5])

    dx = lax.rem(x + XN - z // 2, XN)
    on_lane = core == lax.rem(z, 2)
    is_src = jnp.logical_and(on_lane, dx == 0)
    is_near_src = jnp.logical_and(is_src, far_plane == 0)
    sel = 1 - is_near_src.astype(jnp.int32)

    for i in range(2):
        for j in range(2):
            t2[i * virtual:(i + 1) * virtual, j * virtual:(j + 1) * virtual] = amp[i, j]
    ev_col[...] = jnp.broadcast_to(ev_row[...], (virtual, virtual)).T

    @pl.loop(0, ITERS)
    def _(it):
        first = it == 0

        quarter = side // 4
        theirs = pl.ds(pl.multiple_of(side // 2 + (1 - yh) * quarter, quarter), quarter)
        mine = pl.ds(pl.multiple_of(side // 2 + yh * quarter, quarter), quarter)
        part[it, theirs, :] = nt(t2[theirs, :], fit[...]).astype(BF16)
        for u in (4, 3, 5, 2, 6, 1, 7, 0):
            o = lax.rem(z + u, ZN)
            send(part.at[it, b_rows(1 - yh, o)], yfirst.at[it, o], y_send.at[it], y_sem.at[it, 0, o], y_far)
        @pl.when(first)
        def _():
            f_seed()

        part[it, 0:side // 2, :] = nt(t2[0:side // 2, :], fit[...]).astype(BF16)

        def there(way, steps):
            return lax.rem(z + steps * toward[way], ZN)

        def add_a(at, way, slot, s):
            ref = rsa.at[it, way, slot, s]
            arrived(ref, rsa_sem.at[it, way, slot, s])
            return ref[...].astype(F32)

        def send_a(at, way, slot, s, peer):
            send(part.at[it, at], rsa.at[it, way, slot, s], rs_send.at[it], rsa_sem.at[it, way, slot, s], peer)

        def add_b(way, slot):
            ref = rsb.at[it, way, slot]
            arrived(ref, rsb_sem.at[it, way, slot])
            return ref[...].astype(F32)

        def send_b(at, way, slot, peer):
            send(part.at[it, at], rsb.at[it, way, slot], rs_send.at[it], rsb_sem.at[it, way, slot], peer)

        def both_halves(at, o):
            arrived(yfirst.at[it, o], y_sem.at[it, 0, o])
            return part[it, at, :].astype(F32) + yfirst[it, o].astype(F32)

        for k in range(4):
            for s in range(2):
                for way in (RIGHT, LEFT):
                    long = s == way
                    if k == 0:
                        if long:
                            send_a(a_rows(there(way, 4), s), way, 0, s, ring2[way])
                        send_a(a_rows(there(way, 3), s), way, 1, s, ring[way])
                    elif k < 3:
                        at = a_rows(there(way, 3 - k), s)
                        total = part[it, at, :].astype(F32) + add_a(at, way, k, s)
                        if k == 1 and long:
                            total = total + add_a(at, way, 0, s)
                        part[it, at, :] = total.astype(BF16)
                        send_a(at, way, k + 1, s, ring[way])
            @pl.when(first)
            def _(k=k):
                f_step(2 * k)

            if k == 0:
                part[it, mine, :] = nt(t2[mine, :], fit[...]).astype(BF16)
                acc[...] = jnp.zeros_like(acc)
            for way in (RIGHT, LEFT):
                if k == 1:
                    @pl.when(b_long[way])
                    def _(way=way):
                        o = there(way, 4)
                        at = b_rows(yh, o)
                        part[it, at, :] = both_halves(at, o).astype(BF16)
                        send_b(at, way, 0, ring2[way])

                    o = there(way, 3)
                    at = b_rows(yh, o)
                    part[it, at, :] = both_halves(at, o).astype(BF16)
                    send_b(at, way, 1, ring[way])
                elif k > 1:
                    o = there(way, 4 - k)
                    at = b_rows(yh, o)
                    total = both_halves(at, o) + add_b(way, k - 1)
                    part[it, at, :] = total.astype(BF16)
                    if k == 2:
                        @pl.when(b_long[way])
                        def _(way=way, at=at):
                            part[it, at, :] = (part[it, at, :].astype(F32) + add_b(way, 0)).astype(BF16)
                    send_b(at, way, k, ring[way])

            @pl.when(first)
            def _(k=k):
                f_step(2 * k + 1)
                b_step(k)

        for s in range(2):
            at = a_rows(z, s)
            for way in (RIGHT, LEFT):
                arrived(rsa.at[it, way, 3, s], rsa_sem.at[it, way, 3, s])
            yv[it, s] = (
                part[it, at, :].astype(F32)
                + rsa[it, RIGHT, 3, s].astype(F32)
                + rsa[it, LEFT, 3, s].astype(F32)
            ).astype(BF16)
            send(yv.at[it, s], yr.at[it, s], y_send.at[it], y_sem.at[it, 1, s], y_far)

        @pl.when(first)
        def _():
            f_step(8)

        def own_sends(ref, sems):
            for way in (RIGHT, LEFT):
                send(ref, ref, ag_send.at[it], sems[way], ring[way])

        def to_far(ref, o):
            send(ref, ref, y_send.at[it], y_sem.at[it, 2, o], y_far)

        at = b_rows(yh, z)
        arrived(yfirst.at[it, z], y_sem.at[it, 0, z])
        for way in (RIGHT, LEFT):
            arrived(rsb.at[it, way, 3], rsb_sem.at[it, way, 3])
        pp[it, 0, at, :] = (
            part[it, at, :].astype(F32) + yfirst[it, z].astype(F32)
            + rsb[it, RIGHT, 3].astype(F32) + rsb[it, LEFT, 3].astype(F32)
        ).astype(BF16)
        own_sends(pp.at[it, 0, at], [agb_sem.at[it, way, 0] for way in (RIGHT, LEFT)])
        to_far(pp.at[it, 0, at], z)
        for s in range(2):
            at = a_rows(z, s)
            arrived(yr.at[it, s], y_sem.at[it, 1, s])
            pp[it, 0, at, :] = (yv[it, s].astype(F32) + yr[it, s].astype(F32)).astype(BF16)
            own_sends(pp.at[it, 0, at], [aga_sem.at[it, way, 0, s] for way in (RIGHT, LEFT)])

        def sent_on(ref, way, n, long, sems):
            @pl.when(n < 3)
            def _():
                send(ref, ref, ag_send.at[it], sems(n), ring[way])

            @pl.when(jnp.logical_and(n == 2, long))
            def _():
                send(ref, ref, ag_send.at[it], sems(3), ring2[way])

        @pl.loop(0, 6)
        def _(n):
            @pl.when(jnp.logical_and(n >= 1, n <= 3))
            def _():
                for way in (RIGHT, LEFT):
                    o = lax.rem(z + n * toward[1 - way], ZN)
                    ref = pp.at[it, 0, b_rows(yh, o)]
                    arrived(ref, agb_sem.at[it, way, n - 1])
                    sent_on(ref, way, n, b_long[way], lambda h, way=way: agb_sem.at[it, way, h])
                    to_far(ref, o)
                for s in range(2):
                    for way in (RIGHT, LEFT):
                        o = lax.rem(z + n * toward[1 - way], ZN)
                        ref = pp.at[it, 0, a_rows(o, s)]
                        arrived(ref, aga_sem.at[it, way, n - 1, s])
                        sent_on(ref, way, n, s == way, lambda h, way=way, s=s: aga_sem.at[it, way, h, s])

            @pl.when(n == 3)
            def _():
                o = lax.rem(z + 4, ZN)
                for way in (RIGHT, LEFT):
                    @pl.when(b_long[way])
                    def _(way=way):
                        ref = pp.at[it, 0, b_rows(yh, o)]
                        arrived(ref, agb_sem.at[it, way, 3])
                        to_far(ref, o)
                    arrived(pp.at[it, 0, a_rows(o, way)], aga_sem.at[it, way, 3, way])

            @pl.when(first)
            def _():
                f_step(9 + 2 * n)
                f_over(9 + 2 * n)

            def group(m, act):
                act(lax.rem(z + ZN - m, ZN))

                @pl.when(m >= 1)
                def _():
                    act(lax.rem(z + m, ZN))

                @pl.when(m == 3)
                def _():
                    act(lax.rem(z + 4, ZN))

            @pl.when(jnp.logical_and(is_src, n <= 3))
            def _():
                def act(o):
                    for at, index in (
                        (a_rows(o, far_plane), far_plane * 16 + o),
                        (b_rows(yh, o), far_plane * 16 + 8 + o),
                    ):
                        src, dst, sem = pp.at[it, 0, at], pp.at[it, 1, at], bc_sem.at[it, index]
                        for shift in range(1, XN):
                            send(src, dst, bc_send.at[it, shift], sem, plane_peer(far_plane, shift))

                        @pl.when(far_plane == 1)
                        def _():
                            send(src, dst, bc_send.at[it, 0], sem, plane_peer(1, 0))

                group(n, act)

            m = n - 2 * sel

            @pl.when(jnp.logical_and(on_lane, jnp.logical_and(m >= 0, m <= 3)))
            def _():
                def act(o):
                    for at, index in (
                        (a_rows(o, far_plane), far_plane * 16 + o),
                        (b_rows(yl, o), far_plane * 16 + 8 + o),
                    ):
                        src, dst, sem = pp.at[it, sel, at], pp.at[it, 1, at], bc_sem.at[it, index]

                        @pl.when(sel == 1)
                        def _():
                            arrived(dst, sem)

                        send(src, dst, bc_send.at[it, 4], sem, y_near)
                        send(src, dst, bc_send.at[it, 5], sem, near_mate)
                        send(src, dst, bc_send.at[it, 6], sem, mate)

                group(m, act)

            @pl.when(first)
            def _():
                f_step(10 + 2 * n)
                f_over(10 + 2 * n)
                b_step(n + 4)

            @pl.when(n >= 2)
            def _():
                start = lax.rem(core * 8 + (n - 2) * 4, 16)
                bb = bs[pl.ds(start, 4)].reshape(4 * virtual, virtual)
                for p in range(4):
                    i, j = p // 2, p % 2
                    con[p] = nn(
                        bb, t2[i * virtual:(i + 1) * virtual, j * virtual:(j + 1) * virtual]
                    ).astype(BF16)
                for p in range(4):
                    total = acc[p]
                    for k in range(4):
                        total = total + nt(con[p, k * virtual:(k + 1) * virtual, :], bb[k * virtual:(k + 1) * virtual])
                    acc[p] = total

            @pl.when(n == 5)
            def _():
                for o in range(ZN):
                    arrived(pp.at[it, 0, b_rows(1 - yh, o)], y_sem.at[it, 2, o])

            @pl.when(n >= 4)
            def _():
                i = n - 4
                term = nn(pp[it, 0, pl.ds(pl.multiple_of(i * virtual, virtual), virtual), :], fit[...])
                for j in range(2):
                    acc[2 * i + j] += term[:, j * virtual:(j + 1) * virtual]

        @pl.when(first)
        def _():
            for way in (RIGHT, LEFT):
                for p in range(FP):
                    arrived(f_ref(fr, 1 - yh, way, p), f_sem.at[1, way, p])

        for path in range(2):
            @pl.when(jnp.logical_or(jnp.logical_not(on_lane), far_plane != path))
            def _(path=path):
                for o in range(ZN):
                    arrived(pp.at[it, 1, a_rows(o, path)], bc_sem.at[it, path * 16 + o])
                    half = yh if path == 0 else 1 - yh
                    arrived(pp.at[it, 1, b_rows(half, o)], bc_sem.at[it, path * 16 + 8 + o])

        for i in range(2):
            term = tt(fr[:, i * virtual:(i + 1) * virtual], pp[it, sel])
            for j in range(2):
                total = coul[i, j].astype(F32) + acc[2 * i + j] + term[:, j * virtual:(j + 1) * virtual]
                denominator = (eps[row * 2 + i] + eps[col * 2 + j]) - ev_col[...] - ev_row[...]
                updated = (total / denominator).astype(BF16)
                t2[i * virtual:(i + 1) * virtual, j * virtual:(j + 1) * virtual] = updated
                out[i, j] = updated

        def left(pieces, sem):
            arrived(part.at[it, pl.ds(0, pieces * sub)], sem)

        left(21, rs_send.at[it])
        left(21, ag_send.at[it])
        left(18, y_send.at[it])

        @pl.when(on_lane)
        def _():
            for way in range(4, 7):
                left(16, bc_send.at[it, way])

        @pl.when(is_src)
        def _():
            for way in range(1, 4):
                left(16, bc_send.at[it, way])

            @pl.when(far_plane == 1)
            def _():
                left(16, bc_send.at[it, 0])

    def f_left(pieces, sem):
        arrived(fr.at[pl.ds(0, pieces * f_rows)], sem)

    for way, d in ((RIGHT, d_right), (LEFT, d_left)):
        @pl.when(d < ZN - 1)
        def _(way=way):
            f_left(FP, f_send.at[way])

    @pl.when(jnp.logical_and(is_seed, far_plane == 1))
    def _():
        f_left(2 * FP, f_send.at[2])

    f_left(2 * FP, f_send.at[3])
    arrived(block(x, yl), b_send.at[0])
    arrived(pair(x), b_send.at[1])
    arrived(pair(x), b_send.at[2])
    arrived(block(x, yl), b_send.at[3])
    arrived(block(x, yl), b_send.at[4])
    arrived(bs.at[pl.ds(core * 8, 8)], b_send.at[5])


def body(amplitudes, coulomb, fit_ov, fit_vv, eps_occ, eps_vir):
    occ_local, occ_other, virtual, _ = amplitudes.shape
    aux = fit_ov.shape[0]
    side = occ_local * virtual
    sub = side // (4 * ZN)
    fit = fit_ov.reshape(aux, occ_other * virtual)
    batch = fit_vv.shape[0] * lax.axis_size("row")
    vmem = pl.BlockSpec(memory_space=pltpu.VMEM)
    dma = pltpu.SemaphoreType.DMA
    return pl.pallas_call(
        kernel,
        out_shape=jax.ShapeDtypeStruct(amplitudes.shape, BF16),
        in_specs=[pl.BlockSpec(memory_space=pltpu.SMEM)] + [vmem] * 5,
        out_specs=vmem,
        scratch_shapes=[
            pltpu.VMEM((side, occ_other * virtual), BF16),
            pltpu.VMEM((ITERS, side, aux), BF16),
            pltpu.VMEM((ITERS, 2, 4, 2, sub, aux), BF16),
            pltpu.VMEM((ITERS, 2, 4, sub, aux), BF16),
            pltpu.VMEM((ITERS, ZN, sub, aux), BF16),
            pltpu.VMEM((ITERS, 2, sub, aux), BF16),
            pltpu.VMEM((ITERS, 2, sub, aux), BF16),
            pltpu.VMEM((ITERS, 2, side, aux), BF16),
            pltpu.VMEM((aux, side), BF16),
            pltpu.VMEM((batch, virtual, virtual), BF16),
            pltpu.VMEM((occ_local * occ_other, virtual, virtual), F32),
            pltpu.VMEM((4, 4 * virtual, virtual), BF16),
            pltpu.VMEM((virtual, virtual), F32),
            dma((ITERS, 2, 4, 2)),
            dma((ITERS, 2, 4)),
            dma((ITERS, 3, ZN)),
            dma((ITERS, 2, 4, 2)),
            dma((ITERS, 2, 4)),
            dma((ITERS, 4 * ZN)),
            dma((2, 2, FP)),
            dma((6,)),
            dma((ITERS,)),
            dma((ITERS,)),
            dma((ITERS,)),
            dma((ITERS, 7)),
            dma((4,)),
            dma((6,)),
            dma,
        ],
        compiler_params=pltpu.CompilerParams(
            collective_id=0, has_side_effects=True, vmem_limit_bytes=60 * 2**20
        ),
        name="sweeps",
    )(eps_occ, amplitudes, coulomb, fit, fit_vv, eps_vir[None, :])


def solution(mesh):
    in_specs = (
        P("row", "col", None, None),
        P("row", "col", None, None),
        P(None, "col", None),
        P("row", None, None),
        P(),
        P(),
    )
    out_specs = P("row", "col", None, None)
    return jax.shard_map(body, mesh=mesh, in_specs=in_specs, out_specs=out_specs, check_vma=False)
```

time: 133 us -> 118 us (0.89)
  the two profiles are of different devices: /device:TPU:13 before, /device:TPU:1 now
where the time goes in v3:
time: 118 us
  Pallas kernels  114 us (97%)
  local copies, waits for them, and re-layouts  4.31 us (4%)
    pallas_call x1, Pallas kernels, body(): pl.pallas_call(kernel, out_shape=jax.ShapeDtypeStruct(amplitudes.shape, B...  114 us
    unnamed x2, local copies, waits for them, and re-layouts  4.31 us

profile of v3, /device:TPU:1, one launch (start us, length us, event | category | flops | bytes accessed | tf_op | source)
XLA Modules:
  0.0 117.9 jit_solution(2020005013396690085)
XLA Ops:
  0.0 2.4 %copy.7 = bf16[128,8,2,256]{3,1,2,0:T(8,128)(2,1)} copy(bf16[128,8,2,256]{3,2,1,0:T(2,128)(2,1)} %bitcast.4) | data formatting | bytes 2097152
  2.4 113.6 %sweeps.1 = bf16[2,2,256,256]{3,2,1,0:T(8,128)(2,1)} custom-call(f32[32]{0:T(128)} %eps.1, bf16[2,2,256,256]{3,2,1,0:T(8,128)(2,1)} %amp.1, bf16[2,2,256,256]{3,2,1,0:T(8,128)(2,1)} %coul.1, bf16[1024,512]{1,0:T(8,128)(2,1)} %bitcast.3, bf16[1,256,256]{2,1,0:T(8,128)(2,1)} %own_b.1, f32[1,256]{1,0:T(1,128)} %bitcast.5), custom_call_target="tpu_custom_call" | custom-call | tf_op jit(solution)/shard_map/sweeps/pallas_call | solution.py:528
  116.0 1.9 %copy.9 = bf16[2,2,256,256]{3,2,1,0:T(8,128)(2,1)} copy(bf16[2,2,256,256]{3,2,1,0:T(8,128)(2,1)} %sweeps.1) | data formatting | bytes 1048576

commit v4 on v3

--- a/solution.py
+++ b/solution.py
@@ -13,8 +13,8 @@
 ZN = 8
 XN = 4
 RIGHT, LEFT = 0, 1
-F_OVER = 9
-FP = 4
+F_OVER = 8
+FP = 8
 
 
 def nn(a, b):
@@ -55,7 +55,6 @@
 
     z_next2 = dev(yl, x, core, yh, lax.rem(z + 2, ZN))
     z_prev2 = dev(yl, x, core, yh, lax.rem(z + ZN - 2, ZN))
-    near_mate = dev(1 - yl, x, 1 - core, yh, z)
     far_plane = (yl != yh).astype(jnp.int32)
 
     def plane_peer(flip, shift):
@@ -64,7 +63,7 @@
         return dev(yl_, lax.rem(x + shift, XN), core, yh_, z)
 
     barrier = pltpu.get_barrier_semaphore()
-    peers = [z_next, z_prev, z_next2, z_prev2, y_far, y_near, near_mate, mate]
+    peers = [z_next, z_prev, z_next2, z_prev2, y_far, y_near, mate]
     peers += [plane_peer(0, shift) for shift in range(1, XN)] + [plane_peer(1, shift) for shift in range(XN)]
     for peer in peers:
         pl.semaphore_signal(barrier, inc=1, device_id=peer, device_id_type=MESH)
@@ -239,20 +238,51 @@
             return part[it, at, :].astype(F32) + yfirst[it, o].astype(F32)
 
         for k in range(4):
-            for s in range(2):
+            def round_a(k):
+                for s in range(2):
+                    for way in (RIGHT, LEFT):
+                        long = s == way
+                        if k == 0:
+                            if long:
+                                send_a(a_rows(there(way, 4), s), way, 0, s, ring2[way])
+                            send_a(a_rows(there(way, 3), s), way, 1, s, ring[way])
+                        elif k < 3:
+                            at = a_rows(there(way, 3 - k), s)
+                            total = part[it, at, :].astype(F32) + add_a(at, way, k, s)
+                            if k == 1 and long:
+                                total = total + add_a(at, way, 0, s)
+                            part[it, at, :] = total.astype(BF16)
+                            send_a(at, way, k + 1, s, ring[way])
+            def round_b(k):
                 for way in (RIGHT, LEFT):
-                    long = s == way
-                    if k == 0:
-                        if long:
-                            send_a(a_rows(there(way, 4), s), way, 0, s, ring2[way])
-                        send_a(a_rows(there(way, 3), s), way, 1, s, ring[way])
-                    elif k < 3:
-                        at = a_rows(there(way, 3 - k), s)
-                        total = part[it, at, :].astype(F32) + add_a(at, way, k, s)
-                        if k == 1 and long:
-                            total = total + add_a(at, way, 0, s)
+                    if k == 1:
+                        @pl.when(b_long[way])
+                        def _(way=way):
+                            o = there(way, 4)
+                            at = b_rows(yh, o)
+                            part[it, at, :] = both_halves(at, o).astype(BF16)
+                            send_b(at, way, 0, ring2[way])
+
+                        o = there(way, 3)
+                        at = b_rows(yh, o)
+                        part[it, at, :] = both_halves(at, o).astype(BF16)
+                        send_b(at, way, 1, ring[way])
+                    elif k > 1:
+                        o = there(way, 4 - k)
+                        at = b_rows(yh, o)
+                        total = both_halves(at, o) + add_b(way, k - 1)
                         part[it, at, :] = total.astype(BF16)
-                        send_a(at, way, k + 1, s, ring[way])
+                        if k == 2:
+                            @pl.when(b_long[way])
+                            def _(way=way, at=at):
+                                part[it, at, :] = (part[it, at, :].astype(F32) + add_b(way, 0)).astype(BF16)
+                        send_b(at, way, k, ring[way])
+
+            if k == 0:
+                round_a(k)
+            else:
+                round_b(k)
+
             @pl.when(first)
             def _(k=k):
                 f_step(2 * k)
@@ -260,29 +290,8 @@
             if k == 0:
                 part[it, mine, :] = nt(t2[mine, :], fit[...]).astype(BF16)
                 acc[...] = jnp.zeros_like(acc)
-            for way in (RIGHT, LEFT):
-                if k == 1:
-                    @pl.when(b_long[way])
-                    def _(way=way):
-                        o = there(way, 4)
-                        at = b_rows(yh, o)
-                        part[it, at, :] = both_halves(at, o).astype(BF16)
-                        send_b(at, way, 0, ring2[way])
-
-                    o = there(way, 3)
-                    at = b_rows(yh, o)
-                    part[it, at, :] = both_halves(at, o).astype(BF16)
-                    send_b(at, way, 1, ring[way])
-                elif k > 1:
-                    o = there(way, 4 - k)
-                    at = b_rows(yh, o)
-                    total = both_halves(at, o) + add_b(way, k - 1)
-                    part[it, at, :] = total.astype(BF16)
-                    if k == 2:
-                        @pl.when(b_long[way])
-                        def _(way=way, at=at):
-                            part[it, at, :] = (part[it, at, :].astype(F32) + add_b(way, 0)).astype(BF16)
-                    send_b(at, way, k, ring[way])
+            if k > 0:
+                round_a(k)
 
             @pl.when(first)
             def _(k=k):
@@ -303,6 +312,7 @@
         @pl.when(first)
         def _():
             f_step(8)
+            f_over(8)
 
         def own_sends(ref, sems):
             for way in (RIGHT, LEFT):
@@ -336,6 +346,26 @@
             def _():
                 send(ref, ref, ag_send.at[it], sems(3), ring2[way])
 
+        def group(m, act):
+            act(lax.rem(z + ZN - m, ZN))
+
+            @pl.when(m >= 1)
+            def _():
+                act(lax.rem(z + m, ZN))
+
+            @pl.when(m == 3)
+            def _():
+                act(lax.rem(z + 4, ZN))
+
+        def relay(o):
+            for at, index in (
+                (a_rows(o, 1 - far_plane), (1 - far_plane) * 16 + o),
+                (b_rows(1 - yl, o), (1 - far_plane) * 16 + 8 + o),
+            ):
+                ref, sem = pp.at[it, 1, at], bc_sem.at[it, index]
+                arrived(ref, sem)
+                send(ref, ref, bc_send.at[it, 5], sem, mate)
+
         @pl.loop(0, 6)
         def _(n):
             @pl.when(jnp.logical_and(n >= 1, n <= 3))
@@ -369,17 +399,6 @@
                 f_step(9 + 2 * n)
                 f_over(9 + 2 * n)
 
-            def group(m, act):
-                act(lax.rem(z + ZN - m, ZN))
-
-                @pl.when(m >= 1)
-                def _():
-                    act(lax.rem(z + m, ZN))
-
-                @pl.when(m == 3)
-                def _():
-                    act(lax.rem(z + 4, ZN))
-
             @pl.when(jnp.logical_and(is_src, n <= 3))
             def _():
                 def act(o):
@@ -413,10 +432,15 @@
                             arrived(dst, sem)
 
                         send(src, dst, bc_send.at[it, 4], sem, y_near)
-                        send(src, dst, bc_send.at[it, 5], sem, near_mate)
                         send(src, dst, bc_send.at[it, 6], sem, mate)
 
                 group(m, act)
+
+            @pl.when(jnp.logical_and(on_lane, n >= 4))
+            def _():
+                @pl.loop(n - 4, 2 * n - 7)
+                def _(m):
+                    group(m, relay)
 
             @pl.when(first)
             def _():
@@ -453,12 +477,21 @@
 
         @pl.when(first)
         def _():
+            @pl.loop(21, 26)
+            def _(k):
+                f_step(k)
+                f_over(k)
+
             for way in (RIGHT, LEFT):
                 for p in range(FP):
                     arrived(f_ref(fr, 1 - yh, way, p), f_sem.at[1, way, p])
 
+        @pl.when(on_lane)
+        def _():
+            group(3, relay)
+
         for path in range(2):
-            @pl.when(jnp.logical_or(jnp.logical_not(on_lane), far_plane != path))
+            @pl.when(jnp.logical_not(on_lane))
             def _(path=path):
                 for o in range(ZN):
                     arrived(pp.at[it, 1, a_rows(o, path)], bc_sem.at[it, path * 16 + o])

time: 118 us -> 107 us (0.907)
  Pallas kernels: 114 us -> 102 us
    pallas_call x1, Pallas kernels: 114 us -> 102 us  [body(): pl.pallas_call(kernel, out_shape=jax.ShapeDtypeStruct(amplitudes.shape, B...]
where the time goes in v4:
time: 107 us; the launch traced here: 106 us
  Pallas kernels  102 us (95%)
  local copies, waits for them, and re-layouts  4.31 us (4%)
    pallas_call x1, Pallas kernels, body(): pl.pallas_call(kernel, out_shape=jax.ShapeDtypeStruct(amplitudes.shape, B...  102 us
    unnamed x2, local copies, waits for them, and re-layouts  4.31 us

profile of v4, /device:TPU:1, one launch (start us, length us, event | category | flops | bytes accessed | tf_op | source)
XLA Modules:
  0.0 106.4 jit_solution(13867431139967166909)
XLA Ops:
  0.0 2.4 %copy.7 = bf16[128,8,2,256]{3,1,2,0:T(8,128)(2,1)} copy(bf16[128,8,2,256]{3,2,1,0:T(2,128)(2,1)} %bitcast.4) | data formatting | bytes 2097152
  2.4 102.1 %sweeps.1 = bf16[2,2,256,256]{3,2,1,0:T(8,128)(2,1)} custom-call(f32[32]{0:T(128)} %eps.1, bf16[2,2,256,256]{3,2,1,0:T(8,128)(2,1)} %amp.1, bf16[2,2,256,256]{3,2,1,0:T(8,128)(2,1)} %coul.1, bf16[1024,512]{1,0:T(8,128)(2,1)} %bitcast.3, bf16[1,256,256]{2,1,0:T(8,128)(2,1)} %own_b.1, f32[1,256]{1,0:T(1,128)} %bitcast.5), custom_call_target="tpu_custom_call" | custom-call | tf_op jit(solution)/shard_map/sweeps/pallas_call | solution.py:561
  104.5 1.9 %copy.9 = bf16[2,2,256,256]{3,2,1,0:T(8,128)(2,1)} copy(bf16[2,2,256,256]{3,2,1,0:T(8,128)(2,1)} %sweeps.1) | data formatting | bytes 1048576

commit v5 on v4

--- a/solution.py
+++ b/solution.py
@@ -29,10 +29,10 @@
     return lax.dot_general(a, b, (((0,), (1,)), ((), ())), preferred_element_type=F32)
 
 
-def kernel(eps, amp, coul, fit, own_b, ev_row, out,
+def kernel(eps, amp, coul_hbm, fit, own_b, ev_row, out,
            t2, part, rsa, rsb, yfirst, yv, yr, pp, fr, bs, acc, con, ev_col,
            rsa_sem, rsb_sem, y_sem, aga_sem, agb_sem, bc_sem, f_sem, b_sem,
-           rs_send, y_send, ag_send, bc_send, f_send, b_send, local_sem):
+           rs_send, y_send, ag_send, bc_send, f_send, b_send, local_sem, coul, coul_sem):
     row = lax.axis_index("row")
     col = lax.axis_index("col")
     core = lax.rem(row, 2)
@@ -78,6 +78,8 @@
     def arrived(ref, sem):
         pltpu.make_async_copy(ref, ref, sem).wait()
 
+    exchange = pltpu.make_async_copy(coul_hbm, coul, coul_sem)
+    exchange.start()
     virtual = amp.shape[2]
     side = part.shape[1]
     sub = side // (4 * ZN)
@@ -498,6 +500,10 @@
                     half = yh if path == 0 else 1 - yh
                     arrived(pp.at[it, 1, b_rows(half, o)], bc_sem.at[it, path * 16 + 8 + o])
 
+        @pl.when(first)
+        def _():
+            exchange.wait()
+
         for i in range(2):
             term = tt(fr[:, i * virtual:(i + 1) * virtual], pp[it, sel])
             for j in range(2):
@@ -561,7 +567,7 @@
     return pl.pallas_call(
         kernel,
         out_shape=jax.ShapeDtypeStruct(amplitudes.shape, BF16),
-        in_specs=[pl.BlockSpec(memory_space=pltpu.SMEM)] + [vmem] * 5,
+        in_specs=[pl.BlockSpec(memory_space=pltpu.SMEM)] + [vmem, pl.BlockSpec(memory_space=pl.ANY)] + [vmem] * 3,
         out_specs=vmem,
         scratch_shapes=[
             pltpu.VMEM((side, occ_other * virtual), BF16),
@@ -592,6 +598,8 @@
             dma((4,)),
             dma((6,)),
             dma,
+            pltpu.VMEM(coulomb.shape, BF16),
+            dma,
         ],
         compiler_params=pltpu.CompilerParams(
             collective_id=0, has_side_effects=True, vmem_limit_bytes=60 * 2**20

time: 107 us -> 107 us (level)
  no operation moved by 1% of the time
where the time goes in v5:
time: 107 us; the launch traced here: 106 us
  Pallas kernels  102 us (95%)
  local copies, waits for them, and re-layouts  4.31 us (4%)
    pallas_call x1, Pallas kernels, body(): pl.pallas_call(kernel, out_shape=jax.ShapeDtypeStruct(amplitudes.shape, B...  102 us
    unnamed x2, local copies, waits for them, and re-layouts  4.31 us

profile of v5, /device:TPU:1, one launch (start us, length us, event | category | flops | bytes accessed | tf_op | source)
XLA Modules:
  0.0 106.2 jit_solution(11292202535891971101)
XLA Ops:
  0.0 2.4 %copy.7 = bf16[128,8,2,256]{3,1,2,0:T(8,128)(2,1)} copy(bf16[128,8,2,256]{3,2,1,0:T(2,128)(2,1)} %bitcast.4) | data formatting | bytes 2097152
  2.4 101.8 %sweeps.1 = bf16[2,2,256,256]{3,2,1,0:T(8,128)(2,1)} custom-call(f32[32]{0:T(128)} %eps.1, bf16[2,2,256,256]{3,2,1,0:T(8,128)(2,1)} %amp.1, bf16[2,2,256,256]{3,2,1,0:T(8,128)(2,1)} %coul_hbm.1, bf16[1024,512]{1,0:T(8,128)(2,1)} %bitcast.3, bf16[1,256,256]{2,1,0:T(8,128)(2,1)} %own_b.1, f32[1,256]{1,0:T(1,128)} %bitcast.5), custom_call_target="tpu_custom_call" | custom-call | tf_op jit(solution)/shard_map/sweeps/pallas_call | solution.py:567
  104.3 1.9 %copy.9 = bf16[2,2,256,256]{3,2,1,0:T(8,128)(2,1)} copy(bf16[2,2,256,256]{3,2,1,0:T(8,128)(2,1)} %sweeps.1) | data formatting | bytes 1048576
